TPU v7x, 32 devices: a whole 2x2x4 slice. The times are simulated.
32 devices in a mesh: seg: 8 (over z, y), blk: 4 (over x, core).
Axes of the slice: x: 2, y: 2, z: 4, core: 2. Of those that a mesh axis runs over, the one named last changes fastest.
Arguments:
- strain_rate: bfloat16 [2048, 16384], P('blk', 'seg'), may hold values from -1000 to 1000
- fir_taps: float32 [64], replicated, may hold values from -0.75 to 0.75
Outputs:
- correlation: float32 [2048, 2048, 128], P('blk', 'seg')
All inputs are finite; a program needn't handle non-finite values.
Results may differ from a plain program's by a relative error of at most 0.0023.
Values may be sent and summed in bfloat16 or wider, within the bound.
No kernel may reach another device: no remote copies, remote signals or barrier semaphores. Data moves between devices by JAX's collectives and lax.ppermute only.
A program may use at most 256 MiB of HBM per device.

v0:
```python
import math
import jax
import jax.numpy as jnp
from jax import lax
from jax.sharding import PartitionSpec as P

NFFT = 1024
NBIN = 128
FLO = 8
LAGS = 128
TAPS = 64
RAMW = 32
S_DEV = 2
epsilon = 1e-06


def with_halo(cells, sides, width):
    for axis, dim in sides:
        count = lax.axis_size(axis)
        ends = count - 1
        head = lax.slice_in_dim(cells, 0, width, axis=dim)
        tail = lax.slice_in_dim(cells, cells.shape[dim] - width, cells.shape[dim], axis=dim)
        cells = jnp.concatenate(
            [
                lax.ppermute(tail, axis, [(i, (i + 1) % count) for i in range(ends)]),
                cells,
                lax.ppermute(head, axis, [((i + 1) % count, i) for i in range(ends)]),
            ],
            axis=dim,
        )
    return cells


def broadcast(shard, axis, root):
    mine = lax.axis_index(axis) == root
    return lax.psum(jnp.where(mine, shard, jnp.zeros_like(shard)), axis)


def normalize(extended):
    window_len = 2 * RAMW + 1
    magnitude = jnp.abs(extended)
    running = lax.reduce_window(
        magnitude, jnp.zeros((), extended.dtype), lax.add, (1, window_len), (1, 1), "VALID"
    )
    return extended[:, RAMW : extended.shape[1] - RAMW] / (running / window_len + epsilon)


def band_matrix(fir_taps):
    rows_len = NFFT + TAPS
    padded = jnp.concatenate([fir_taps, jnp.zeros((rows_len + 2 - TAPS,), fir_taps.dtype)])
    tiled = jnp.tile(padded, NFFT // 2)[: NFFT // 2 * rows_len]
    return tiled.reshape(NFFT // 2, rows_len).T


def filter_blocks(normed, fir_taps):
    channels = normed.shape[0]
    groups = (normed.shape[1] - TAPS) // NFFT
    leading = normed[:, : groups * NFFT].reshape(channels, groups, NFFT)
    trailing = jnp.concatenate([leading[:, 1:, :TAPS], normed[:, None, groups * NFFT :]], axis=1)
    framed = jnp.concatenate([leading, trailing], axis=2)
    return jnp.einsum("cgw,wu->cgu", framed, band_matrix(fir_taps), precision=lax.Precision.HIGHEST)


def dft_table():
    sample_index = jnp.arange(NFFT, dtype=jnp.int32)[:, None]
    freq_index = jnp.arange(NBIN, dtype=jnp.int32)[None, :] + FLO
    phase_arg = (sample_index * freq_index % NFFT).astype(jnp.float32) * (2 * math.pi / NFFT)
    norm_scale = 1.0 / math.sqrt(NFFT)
    stacked = jnp.stack([jnp.cos(phase_arg) * norm_scale, -jnp.sin(phase_arg) * norm_scale], axis=2)
    return stacked.reshape(NFFT, 2 * NBIN)


def lag_table():
    freq_index = jnp.arange(NBIN, dtype=jnp.int32)[:, None] + FLO
    lag_index = jnp.arange(LAGS, dtype=jnp.int32)[None, :]
    phase_arg = (freq_index * lag_index % NFFT).astype(jnp.float32) * (2 * math.pi / NFFT)
    return jnp.cos(phase_arg)


def shards(strain_rate, fir_taps):
    channels, own_time = strain_rate.shape
    margin = RAMW + TAPS // 2
    reach_len = NFFT + margin
    widened = with_halo(strain_rate, (("seg", 1),), reach_len)
    extended = widened[:, reach_len - margin :].astype(jnp.float32)
    halves = filter_blocks(normalize(extended), fir_taps)
    dft_cols = dft_table()
    early_half = jnp.einsum(
        "csh,hk->ksc", halves[:, :-1], dft_cols[: NFFT // 2], precision=lax.Precision.HIGHEST
    )
    late_half = jnp.einsum(
        "csh,hk->ksc", halves[:, 1:], dft_cols[NFFT // 2 :], precision=lax.Precision.HIGHEST
    )
    spectra = (early_half + late_half).astype(jnp.bfloat16).reshape(NBIN, 2, S_DEV, channels)
    segs_total = S_DEV * lax.axis_size("seg")
    lag_cos = lag_table()
    gathered = lax.all_gather(spectra, "seg", axis=2, tiled=True)
    part_width = channels * lax.axis_size("blk") // lax.axis_size("seg")
    first_col = lax.axis_index("seg") * part_width
    source_block = broadcast(gathered, "blk", first_col // channels)
    partner = lax.dynamic_slice_in_dim(source_block, first_col % channels, part_width, 3)
    cross_spec = (
        jnp.einsum("fpsi,fpsj->fij", gathered, partner, preferred_element_type=jnp.float32)
        / segs_total
    )
    correlation = (
        jnp.einsum("fij,fl->ijl", cross_spec, lag_cos, precision=lax.Precision.HIGHEST) / NBIN
    )
    return correlation


def solution(mesh):
    return jax.shard_map(
        shards,
        mesh=mesh,
        in_specs=(P("blk", "seg"), P()),
        out_specs=P("blk", "seg", None),
        check_vma=False,
    )
```

profile of v0, /device:TPU:0, one launch (start us, length us, event | category | flops | bytes accessed | tf_op | source)
XLA Modules:
  0.0 578.1 jit_solution(5507240948475038173)
XLA Ops:
  6.5 2.9 copy.27
  10.9 5.1 collective-permute-start
  17.3 2.1 cosine_multiply_fusion
  20.4 2.0 copy.26
  22.4 2.2 reshape.133
  24.6 2.0 copy.31
  26.7 2.2 reshape.134
  30.5 4.5 tile.10
  34.9 3.1 slice.64
  38.1 3.4 reshape.130
  41.4 22.5 %collective-permute-done = bf16[512,1088]{0,1:T(8,128)(2,1)S(1)} collective-permute-done((bf16[512,1088]{0,1:T(8,128)(2,1)}, bf16[512,1088]{0,1:T(8,128)(2,1)S(1)}, u32[]{:S(2)}, u32[]{:S(2)}) %collective-permute-start) | collective-permute-done | bytes 1114144 | tf_op jit(solution)/shard_map/ppermute | solution.py:25
  63.9 5.0 fusion.56
  68.9 120.4 %reduce_window.7 = f32[512,3136]{0,1:T(8,128)} reduce-window(f32[512,3200]{0,1:T(8,128)} %fusion.56, f32[]{:T(128)} %constant.69.clone.1), window={size=1x65}, to_apply=%region_0.0 | reduce-window | flops 102760448 | bytes 12976132 | tf_op jit(solution)/shard_map/reduce_window | solution.py:42
  189.3 2.3 fusion.11
  192.5 4.4 slice_divide_fusion
  197.8 3.6 slice.61
  201.5 24.3 %fusion.4 = f32[512,3,512]{2,0,1:T(8,128)S(1)} fusion(f32[512,1,64]{0,2,1:T(8,128)S(1)} %slice_bitcast_fusion, f32[512,2,64]{0,2,1:T(8,128)S(1)} %slice.62, f32[512,3,1024]{0,2,1:T(8,128)S(1)} %bitcast.25, f32[512,1088]{1,0:T(8,128)S(1)} %copy-done.1), kind=kOutput, calls=%fused_computation.4 | convolution fusion | flops 10270998528 | bytes 12058624 | tf_op jit(solution)/shard_map/cgw,wu->cgu/dot_general | solution.py:61
  225.8 1.9 fusion.13
  227.8 1.9 fusion.24
  230.9 75.6 %all-gather.2.cloned.1.call-done = bf16[128,2,16,512]{3,0,1,2:T(8,128)(2,1)} async-done(((bf16[128,2,2,512]{3,0,1,2:T(8,128)(2,1)}), bf16[128,2,16,512]{3,0,1,2:T(8,128)(2,1)}) %all-gather.2.cloned.1.call-update) | async-done | bytes 4194320 | tf_op jit(solution)/shard_map/all_gather | solution.py:97
  306.5 6.6 %broadcast_select_fusion = bf16[128,2,16,512]{3,2,1,0:T(8,128)(2,1)} fusion(pred[]{:T(512)S(6)} %eq.9, bf16[128,2,16,512]{3,0,1,2:T(8,128)(2,1)} %all-gather.2.cloned.1.call-done), kind=kLoop, calls=%fused_computation.11 | loop fusion | flops 2097152 | bytes 8388609 | tf_op jit(solution)/shard_map/jit(_where)/select_n | solution.py:36
  313.2 83.9 %all-reduce.3.cloned.1.call-done = bf16[128,2,16,512]{3,2,1,0:T(8,128)(2,1)} async-done(((bf16[128,2,16,512]{3,2,1,0:T(8,128)(2,1)}), bf16[128,2,16,512]{3,2,1,0:T(8,128)(2,1)}) %all-reduce.3.cloned.1.call-update) | async-done | bytes 4194320 | tf_op jit(solution)/shard_map/psum | solution.py:36
  397.1 25.8 %bitcast_multiply_fusion = f32[128,512,256]{2,1,0:T(8,128)} fusion(bf16[128,2,16,512]{3,0,1,2:T(8,128)(2,1)} %all-gather.2.cloned.1.call-done, bf16[128,2,16,512]{3,2,1,0:T(8,128)(2,1)} %all-reduce.3.cloned.1.call-done, s32[]{:T(128)S(6)} %select_n.52), kind=kOutput, calls=%fused_computation | convolution fusion | flops 1090519040 | bytes 73400320 | tf_op jit(solution)/shard_map/fpsi,fpsj->fij/dot_general | solution.py:103
  422.9 148.2 %broadcast_multiply_fusion = f32[512,256,128]{2,1,0:T(8,128)} fusion(f32[128,512,256]{2,1,0:T(8,128)} %bitcast_multiply_fusion, s32[128]{0:T(128)S(1)} %iota_add_fusion), kind=kOutput, calls=%fused_computation.3 | convolution fusion | flops 25786810368 | bytes 134218240 | tf_op jit(solution)/shard_map/fij,fl->ijl/dot_general | solution.py:107
  (25 shorter events, 8.3 us)
Async XLA Ops:
  6.5 300.0 %all-gather.2.cloned.1.call-start = ((), (), s32[]{:S(2)}) async-start(), calls=%async_computation | async-start | bytes 4718592 | tf_op jit(solution)/shard_map/all_gather | solution.py:97
  10.9 18.0 %copy-start.4 = (f32[64]{0:T(128)S(1)}, f32[64]{0:T(128)}, u32[]{:S(2)}) copy-start(f32[64]{0:T(128)} %param.3) | copy-start | bytes 772
  10.9 53.0 %collective-permute-start = (bf16[512,1088]{0,1:T(8,128)(2,1)}, bf16[512,1088]{0,1:T(8,128)(2,1)S(1)}, u32[]{:S(2)}, u32[]{:S(2)}) collective-permute-start(bf16[512,1088]{0,1:T(8,128)(2,1)} %get-tuple-element.5), channel_id=1, source_target_pairs={{0,4},{4,8},{8,12},{12,16},{16,20},{20,24},{24,28},{1,5},{5,9},{9,... | collective-permute-start | bytes 3342344 | tf_op jit(solution)/shard_map/ppermute | solution.py:25
  16.0 47.9 %collective-permute-start.1 = (bf16[512,1088]{0,1:T(8,128)(2,1)}, bf16[512,1088]{0,1:T(8,128)(2,1)}, u32[]{:S(2)}, u32[]{:S(2)}) collective-permute-start(bf16[512,1088]{0,1:T(8,128)(2,1)} %get-tuple-element.6), channel_id=1, source_target_pairs={{4,0},{8,4},{12,8},{16,12},{20,16},{24,20},{28,24},{5,1},{9,5},{13... | collective-permute-start | bytes 3342344 | tf_op jit(solution)/shard_map/ppermute | solution.py:27
  189.3 3.2 copy-start
  197.8 3.7 copy-start.1
  201.5 24.4 %copy-start.2 = (f32[512,256,1]{0,1,2:T(8,128)S(1)}, f32[512,256,1]{0,1,2:T(8,128)}, u32[]{:S(2)}) copy-start(f32[512,256,1]{0,1,2:T(8,128)} %reshape.134) | copy-start | bytes 1572868
  201.5 26.3 %copy-start.3 = (f32[512,256,1]{0,1,2:T(8,128)S(1)}, f32[512,256,1]{0,1,2:T(8,128)}, u32[]{:S(2)}) copy-start(f32[512,256,1]{0,1,2:T(8,128)} %reshape.133) | copy-start | bytes 1572868
  230.8 166.3 %all-reduce.3.cloned.1.call-start = ((), (), s32[]{:S(2)}) async-start(), calls=%async_computation.1 | async-start | bytes 8388608 | tf_op jit(solution)/shard_map/psum | solution.py:36
Sparse Core Ops, SparseCore 0:
  231.0 75.5 all-gather.1
  313.3 83.7 all-reduce.2
where the time goes:
time: 584 us; the launch traced here: 578 us
  matrix products  202 us (35%)
  waiting for transfers between devices  182 us (31%)
  other arithmetic  142 us (24%)
  local copies, waits for them, and re-layouts  31.8 us (5%)
  between operations  13.8 us (2%)
  starting transfers between devices  6.4 us (1%)
    dot_general x1, matrix products, shards(): jnp.einsum('fij,fl->ijl', cross_spec, lag_cos, precision=lax.Precision.HI...  148 us
    another operation x1, other arithmetic, normalize(): lax.reduce_window(magnitude, jnp.zeros((), extended.dtype), lax.add, (1,...  120 us
    psum x1, waiting for transfers between devices, broadcast(): return lax.psum(jnp.where(mine, shard, jnp.zeros_like(shard)), axis)  83.9 us
    all_gather x1, waiting for transfers between devices, shards(): gathered = lax.all_gather(spectra, 'seg', axis=2, tiled=True)  75.6 us
    dot_general x1, matrix products, shards(): jnp.einsum('fpsi,fpsj->fij', gathered, partner, preferred_element_type=jn...  25.8 us
    dot_general x1, matrix products, filter_blocks(): jnp.einsum('cgw,wu->cgu', framed, band_matrix(fir_taps), precision=lax.Pr...  24.3 us
    ppermute x1, waiting for transfers between devices, with_halo(): lax.ppermute(tail, axis, [(i, (i + 1) % count) for i in range(ends)])  22.5 us
  transfers between devices with their start and end apart: 4, of which 3 were waited for; matrix products, arithmetic and copies ran while one was open for 4% of the time, Pallas kernels for 0%

commit v1 on v0

--- a/solution.py
+++ b/solution.py
@@ -12,6 +12,12 @@
 RAMW = 32
 S_DEV = 2
 epsilon = 1e-06
+
+
+def in_order(parts, dim):
+    shape = list(parts.shape[1:])
+    shape[dim] *= parts.shape[0]
+    return jnp.moveaxis(parts, 0, dim).reshape(shape)
 
 
 def with_halo(cells, sides, width):
@@ -94,7 +100,19 @@
     spectra = (early_half + late_half).astype(jnp.bfloat16).reshape(NBIN, 2, S_DEV, channels)
     segs_total = S_DEV * lax.axis_size("seg")
     lag_cos = lag_table()
-    gathered = lax.all_gather(spectra, "seg", axis=2, tiled=True)
+    size = lax.axis_size("seg")
+    pairs = [(i_2, (i_2 + 1) % size) for i_2 in range(size)]
+    back = [(b, a) for a, b in pairs]
+    lower, upper = ([], [])
+    for step in range(size - 1):
+        if step % 2 == 0:
+            lower.append(lax.ppermute(lower[-1] if lower else spectra, "seg", pairs))
+        else:
+            upper.append(lax.ppermute(upper[-1] if upper else spectra, "seg", back))
+    parts = jnp.stack([*lower[::-1], spectra, *upper])
+    shift = lax.axis_index("seg") - len(lower)
+    parts = parts[(jnp.arange(size) - shift) % size]
+    gathered = in_order(parts, 2)
     part_width = channels * lax.axis_size("blk") // lax.axis_size("seg")
     first_col = lax.axis_index("seg") * part_width
     source_block = broadcast(gathered, "blk", first_col // channels)

time: 584 us -> 621 us (1.063)
  local copies, waits for them, and re-layouts: 31.8 us -> 54.6 us
  starting transfers between devices: 6.4 us -> 21.2 us
    all_gather x1 -> x0, waiting for transfers between devices: 75.6 us -> none  [shards(): gathered = lax.all_gather(spectra, 'seg', axis=2, tiled=True)]
    ppermute x0 -> x7, waiting for transfers between devices: none -> 63.8 us  [the longest x4 52.1 us: shards(): lower.append(lax.ppermute(lower[-1] if lower else spectra, 'seg', pairs))]
    ppermute x0 -> x7, starting transfers between devices: none -> 14.9 us  [the longest x3 9.95 us: shards(): upper.append(lax.ppermute(upper[-1] if upper else spectra, 'seg', back))]
    gather x0 -> x1, local copies, waits for them, and re-layouts: none -> 12.1 us  [shards(): parts = parts[(jnp.arange(size) - shift) % size]]
    psum x1, waiting for transfers between devices: 83.9 us -> 94.3 us  [broadcast(): return lax.psum(jnp.where(mine, shard, jnp.zeros_like(shard)), axis)]
    unnamed x11 -> x18, local copies, waits for them, and re-layouts: 3.7 us -> 13.9 us
  transfers between devices with their start and end apart: 4 -> 10, of which waited for: 3 -> 9; matrix products, arithmetic and copies ran while one was open for 4% -> 6% of each run, Pallas kernels for 0% -> 0%
where the time goes in v1:
time: 621 us; the launch traced here: 614 us
  matrix products  202 us (33%)
  waiting for transfers between devices  181 us (29%)
  other arithmetic  142 us (23%)
  local copies, waits for them, and re-layouts  54.6 us (9%)
  starting transfers between devices  21.2 us (3%)
  between operations  14 us (2%)
    dot_general x1, matrix products, shards(): jnp.einsum('fij,fl->ijl', cross_spec, lag_cos, precision=lax.Precision.HI...  148 us
    another operation x1, other arithmetic, normalize(): lax.reduce_window(magnitude, jnp.zeros((), extended.dtype), lax.add, (1,...  120 us
    psum x1, waiting for transfers between devices, broadcast(): return lax.psum(jnp.where(mine, shard, jnp.zeros_like(shard)), axis)  94.3 us
    ppermute x4, waiting for transfers between devices, shards(): lower.append(lax.ppermute(lower[-1] if lower else spectra, 'seg', pairs))  52.1 us
    dot_general x1, matrix products, shards(): jnp.einsum('fpsi,fpsj->fij', gathered, partner, preferred_element_type=jn...  25.8 us
    dot_general x1, matrix products, filter_blocks(): jnp.einsum('cgw,wu->cgu', framed, band_matrix(fir_taps), precision=lax.Pr...  24.2 us
    ppermute x1, waiting for transfers between devices, with_halo(): lax.ppermute(tail, axis, [(i, (i + 1) % count) for i in range(ends)])  22.5 us
    unnamed x18, local copies, waits for them, and re-layouts  13.9 us
  transfers between devices with their start and end apart: 10, of which 9 were waited for; matrix products, arithmetic and copies ran while one was open for 6% of the time, Pallas kernels for 0%

profile of v1, /device:TPU:0, one launch (start us, length us, event | category | flops | bytes accessed | tf_op | source)
XLA Modules:
  0.0 614.4 jit_solution(14814174991692401973)
XLA Ops:
  6.5 2.9 copy.17
  10.9 5.1 collective-permute-start
  30.5 4.5 tile.10
  35.0 3.1 slice.66
  38.1 3.4 reshape.182
  41.5 22.5 %collective-permute-done = bf16[512,1088]{0,1:T(8,128)(2,1)S(1)} collective-permute-done((bf16[512,1088]{0,1:T(8,128)(2,1)}, bf16[512,1088]{0,1:T(8,128)(2,1)S(1)}, u32[]{:S(2)}, u32[]{:S(2)}) %collective-permute-start) | collective-permute-done | bytes 1114144 | tf_op jit(solution)/shard_map/ppermute | solution.py:31
  63.9 5.0 fusion.58
  68.9 120.5 %reduce_window.7 = f32[512,3136]{0,1:T(8,128)} reduce-window(f32[512,3200]{0,1:T(8,128)} %fusion.58, f32[]{:T(128)} %constant.85.clone.1), window={size=1x65}, to_apply=%region_0.0 | reduce-window | flops 102760448 | bytes 12976132 | tf_op jit(solution)/shard_map/reduce_window | solution.py:48
  192.6 4.4 slice_divide_fusion
  197.8 3.6 slice.63
  201.6 24.2 %fusion.4 = f32[512,3,512]{2,0,1:T(8,128)S(1)} fusion(f32[512,1,64]{0,2,1:T(8,128)S(1)} %slice_bitcast_fusion, f32[512,2,64]{0,2,1:T(8,128)S(1)} %slice.64, f32[512,3,1024]{0,2,1:T(8,128)S(1)} %bitcast.48, f32[512,1088]{1,0:T(8,128)S(1)} %copy-done.1), kind=kOutput, calls=%fused_computation.5 | convolution fusion | flops 10270998528 | bytes 12058624 | tf_op jit(solution)/shard_map/cgw,wu->cgu/dot_general | solution.py:67
  232.4 14.2 %collective-permute-done.2 = bf16[128,2,2,512]{3,1,0,2:T(2,128)(2,1)S(1)} collective-permute-done((bf16[128,2,2,512]{3,1,0,2:T(2,128)(2,1)S(1)}, bf16[128,2,2,512]{3,1,0,2:T(2,128)(2,1)S(1)}, u32[]{:S(2)}, u32[]{:S(2)}) %collective-permute-start.2) | collective-permute-done | bytes 524320 | tf_op jit(solution)/shard_map/ppermute | solution.py:109
  246.5 4.7 collective-permute-start.6
  251.2 17.3 %collective-permute-done.3 = bf16[128,2,2,512]{3,1,0,2:T(2,128)(2,1)S(1)} collective-permute-done((bf16[128,2,2,512]{3,1,0,2:T(2,128)(2,1)S(1)}, bf16[128,2,2,512]{3,1,0,2:T(2,128)(2,1)S(1)}, u32[]{:S(2)}, u32[]{:S(2)}) %collective-permute-start.3) | collective-permute-done | bytes 524320 | tf_op jit(solution)/shard_map/ppermute | solution.py:109
  268.6 2.5 collective-permute-start.4
  274.1 10.8 %collective-permute-done.4 = bf16[128,2,2,512]{3,1,0,2:T(2,128)(2,1)} collective-permute-done((bf16[128,2,2,512]{3,1,0,2:T(2,128)(2,1)S(1)}, bf16[128,2,2,512]{3,1,0,2:T(2,128)(2,1)}, u32[]{:S(2)}, u32[]{:S(2)}) %collective-permute-start.4) | collective-permute-done | bytes 524320 | tf_op jit(solution)/shard_map/ppermute | solution.py:109
  285.2 10.0 %collective-permute-done.7 = bf16[128,2,2,512]{3,1,0,2:T(2,128)(2,1)S(1)} collective-permute-done((bf16[128,2,2,512]{3,1,0,2:T(2,128)(2,1)S(1)}, bf16[128,2,2,512]{3,1,0,2:T(2,128)(2,1)S(1)}, u32[]{:S(2)}, u32[]{:S(2)}) %collective-permute-start.7) | collective-permute-done | bytes 524320 | tf_op jit(solution)/shard_map/ppermute | solution.py:111
  295.2 2.9 collective-permute-start.8
  298.1 9.8 %collective-permute-done.5 = bf16[128,2,2,512]{3,1,0,2:T(2,128)(2,1)} collective-permute-done((bf16[128,2,2,512]{3,1,0,2:T(2,128)(2,1)}, bf16[128,2,2,512]{3,1,0,2:T(2,128)(2,1)}, u32[]{:S(2)}, u32[]{:S(2)}) %collective-permute-start.5) | collective-permute-done | bytes 524320 | tf_op jit(solution)/shard_map/ppermute | solution.py:109
  320.1 12.1 %gather_fusion = bf16[8,128,2,2,512]{4,2,1,3,0:T(2,128)(2,1)} fusion(bf16[8,128,2,2,512]{4,2,1,3,0:T(2,128)(2,1)} %bitcast_dynamic-update-slice_fusion, s32[1024]{0:T(1024)S(1)} %pad_clamp_fusion), kind=kCustom, calls=%fused_computation | custom fusion | bytes 8388640 | tf_op jit(solution)/shard_map/gather | solution.py:114
  332.2 6.6 %broadcast_select_fusion = bf16[128,2,16,512]{3,2,1,0:T(8,128)(2,1)} fusion(pred[]{:T(512)S(6)} %eq.11, bf16[128,2,16,512]{3,1,0,2:T(2,128)(2,1)} %bitcast.45), kind=kLoop, calls=%fused_computation.12 | loop fusion | flops 2097152 | bytes 8388609 | tf_op jit(solution)/shard_map/jit(_where)/select_n | solution.py:42
  338.9 94.3 %all-reduce.3.cloned.1.call-done = bf16[128,2,16,512]{3,2,1,0:T(8,128)(2,1)} async-done(((bf16[128,2,16,512]{3,2,1,0:T(8,128)(2,1)}), bf16[128,2,16,512]{3,2,1,0:T(8,128)(2,1)}) %all-reduce.3.cloned.1.call-update) | async-done | bytes 4194320 | tf_op jit(solution)/shard_map/psum | solution.py:42
  433.2 25.8 %bitcast_multiply_fusion = f32[128,512,256]{2,1,0:T(8,128)} fusion(bf16[128,2,16,512]{3,1,0,2:T(2,128)(2,1)} %bitcast.46, bf16[128,2,16,512]{3,2,1,0:T(8,128)(2,1)} %all-reduce.3.cloned.1.call-done, s32[]{:T(128)S(6)} %select_n.77), kind=kOutput, calls=%fused_computation.1 | convolution fusion | flops 1090519040 | bytes 73400320 | tf_op jit(solution)/shard_map/fpsi,fpsj->fij/dot_general | solution.py:121
  459.0 148.2 %broadcast_multiply_fusion = f32[512,256,128]{2,1,0:T(8,128)} fusion(f32[128,512,256]{2,1,0:T(8,128)} %bitcast_multiply_fusion, s32[128]{0:T(128)S(1)} %iota_add_fusion), kind=kOutput, calls=%fused_computation.4 | convolution fusion | flops 25786810368 | bytes 134218240 | tf_op jit(solution)/shard_map/fij,fl->ijl/dot_general | solution.py:125
  (47 shorter events, 42.1 us)
Async XLA Ops:
  6.5 426.7 %all-reduce.3.cloned.1.call-start = ((), (), s32[]{:S(2)}) async-start(), calls=%async_computation | async-start | bytes 8388608 | tf_op jit(solution)/shard_map/psum | solution.py:42
  10.9 18.0 %copy-start.4 = (f32[64]{0:T(128)S(1)}, f32[64]{0:T(128)}, u32[]{:S(2)}) copy-start(f32[64]{0:T(128)} %param.3) | copy-start | bytes 772
  10.9 53.0 %collective-permute-start = (bf16[512,1088]{0,1:T(8,128)(2,1)}, bf16[512,1088]{0,1:T(8,128)(2,1)S(1)}, u32[]{:S(2)}, u32[]{:S(2)}) collective-permute-start(bf16[512,1088]{0,1:T(8,128)(2,1)} %get-tuple-element.5), channel_id=1, source_target_pairs={{0,4},{4,8},{8,12},{12,16},{16,20},{20,24},{24,28},{1,5},{5,9},{9,... | collective-permute-start | bytes 3342344 | tf_op jit(solution)/shard_map/ppermute | solution.py:31
  16.0 47.9 %collective-permute-start.1 = (bf16[512,1088]{0,1:T(8,128)(2,1)}, bf16[512,1088]{0,1:T(8,128)(2,1)}, u32[]{:S(2)}, u32[]{:S(2)}) collective-permute-start(bf16[512,1088]{0,1:T(8,128)(2,1)} %get-tuple-element.6), channel_id=1, source_target_pairs={{4,0},{8,4},{12,8},{16,12},{20,16},{24,20},{28,24},{5,1},{9,5},{13... | collective-permute-start | bytes 3342344 | tf_op jit(solution)/shard_map/ppermute | solution.py:33
  189.4 3.2 copy-start
  197.8 3.7 copy-start.1
  201.5 24.3 %copy-start.2 = (f32[512,256,1]{0,1,2:T(8,128)S(1)}, f32[512,256,1]{0,1,2:T(8,128)}, u32[]{:S(2)}) copy-start(f32[512,256,1]{0,1,2:T(8,128)} %reshape.195) | copy-start | bytes 1572868
  201.5 26.2 %copy-start.3 = (f32[512,256,1]{0,1,2:T(8,128)S(1)}, f32[512,256,1]{0,1,2:T(8,128)}, u32[]{:S(2)}) copy-start(f32[512,256,1]{0,1,2:T(8,128)} %reshape.194) | copy-start | bytes 1572868
  229.9 16.6 %collective-permute-start.2 = (bf16[128,2,2,512]{3,1,0,2:T(2,128)(2,1)S(1)}, bf16[128,2,2,512]{3,1,0,2:T(2,128)(2,1)S(1)}, u32[]{:S(2)}, u32[]{:S(2)}) collective-permute-start(bf16[128,2,2,512]{3,1,0,2:T(2,128)(2,1)S(1)} %reshape.183), channel_id=1, source_target_pairs={{0,4},{4,8},{8,12},{12,16},{16,20},{20,24},{24,28},{28,0},{1,5},{5... | collective-permute-start | bytes 1572872 | tf_op jit(solution)/shard_map/ppermute | solution.py:109
  246.5 22.0 %collective-permute-start.3 = (bf16[128,2,2,512]{3,1,0,2:T(2,128)(2,1)S(1)}, bf16[128,2,2,512]{3,1,0,2:T(2,128)(2,1)S(1)}, u32[]{:S(2)}, u32[]{:S(2)}) collective-permute-start(bf16[128,2,2,512]{3,1,0,2:T(2,128)(2,1)S(1)} %collective-permute-done.2), channel_id=1, source_target_pairs={{0,4},{4,8},{8,12},{12,16},{16,20},{20,24},{24,28},{28,0},{1,5},{5... | collective-permute-start | bytes 1572872 | tf_op jit(solution)/shard_map/ppermute | solution.py:109
  246.5 25.3 %collective-permute-start.6 = (bf16[128,2,2,512]{3,1,0,2:T(2,128)(2,1)S(1)}, bf16[128,2,2,512]{3,1,0,2:T(2,128)(2,1)S(1)}, u32[]{:S(2)}, u32[]{:S(2)}) collective-permute-start(bf16[128,2,2,512]{3,1,0,2:T(2,128)(2,1)S(1)} %reshape.183), channel_id=1, source_target_pairs={{4,0},{8,4},{12,8},{16,12},{20,16},{24,20},{28,24},{0,28},{5,1},{9... | collective-permute-start | bytes 1572872 | tf_op jit(solution)/shard_map/ppermute | solution.py:111
  268.6 16.4 %collective-permute-start.4 = (bf16[128,2,2,512]{3,1,0,2:T(2,128)(2,1)S(1)}, bf16[128,2,2,512]{3,1,0,2:T(2,128)(2,1)}, u32[]{:S(2)}, u32[]{:S(2)}) collective-permute-start(bf16[128,2,2,512]{3,1,0,2:T(2,128)(2,1)S(1)} %collective-permute-done.3), channel_id=1, source_target_pairs={{0,4},{4,8},{8,12},{12,16},{16,20},{20,24},{24,28},{28,0},{1,5},{5... | collective-permute-start | bytes 1572872 | tf_op jit(solution)/shard_map/ppermute | solution.py:109
  271.8 23.4 %collective-permute-start.7 = (bf16[128,2,2,512]{3,1,0,2:T(2,128)(2,1)S(1)}, bf16[128,2,2,512]{3,1,0,2:T(2,128)(2,1)S(1)}, u32[]{:S(2)}, u32[]{:S(2)}) collective-permute-start(bf16[128,2,2,512]{3,1,0,2:T(2,128)(2,1)S(1)} %collective-permute-done.6), channel_id=1, source_target_pairs={{4,0},{8,4},{12,8},{16,12},{20,16},{24,20},{28,24},{0,28},{5,1},{9... | collective-permute-start | bytes 1572872 | tf_op jit(solution)/shard_map/ppermute | solution.py:111
  285.0 23.0 %collective-permute-start.5 = (bf16[128,2,2,512]{3,1,0,2:T(2,128)(2,1)}, bf16[128,2,2,512]{3,1,0,2:T(2,128)(2,1)}, u32[]{:S(2)}, u32[]{:S(2)}) collective-permute-start(bf16[128,2,2,512]{3,1,0,2:T(2,128)(2,1)} %collective-permute-done.4), channel_id=1, source_target_pairs={{0,4},{4,8},{8,12},{12,16},{16,20},{20,24},{24,28},{28,0},{1,5},{5... | collective-permute-start | bytes 1572872 | tf_op jit(solution)/shard_map/ppermute | solution.py:109
  295.2 23.8 %collective-permute-start.8 = (bf16[128,2,2,512]{3,1,0,2:T(2,128)(2,1)S(1)}, bf16[128,2,2,512]{3,1,0,2:T(2,128)(2,1)S(1)}, u32[]{:S(2)}, u32[]{:S(2)}) collective-permute-start(bf16[128,2,2,512]{3,1,0,2:T(2,128)(2,1)S(1)} %collective-permute-done.7), channel_id=1, source_target_pairs={{4,0},{8,4},{12,8},{16,12},{20,16},{24,20},{28,24},{0,28},{5,1},{9... | collective-permute-start | bytes 1572872 | tf_op jit(solution)/shard_map/ppermute | solution.py:111
Sparse Core Ops, SparseCore 0:
  339.0 94.1 all-reduce.2
